TPU v7x, 512 devices: a whole 4x4x16 slice. The times are simulated.
512 devices in a mesh: lat: 16 (over z_hi, y), lon: 32 (over z_lo, x, core).
Axes of the slice: x: 4, y: 4, z: 16 (z_hi: 4, z_lo: 4; z = z_hi * 4 + z_lo), core: 2. Of those that a mesh axis runs over, the one named last changes fastest.
Arguments:
- queries: float32 [64, 1024, 512], P('lat', 'lon'), may hold values from -80 to 80
- key_rows: float32 [512, 512], P(('lat', 'lon')), may hold values from -8 to 8
- value_rows: float32 [512, 512], P(('lat', 'lon')), may hold values from -6 to 6
- cotangent: float32 [64, 1024, 512], P('lat', 'lon'), may hold values from -25 to 25
- conv_taps: float32 [9, 512], replicated, may hold values from -1.75 to 1.75
Outputs:
- query_grad: float32 [64, 1024, 512], P('lat', 'lon')
- key_grad: float32 [512, 512], P(('lat', 'lon'))
- value_grad: float32 [512, 512], P(('lat', 'lon'))
- tap_update: float32 [9, 512], replicated
All inputs are finite; a program needn't handle non-finite values.
Results may differ from a plain program's by a relative error of at most 0.0003.
Values sent between devices are 32-bit elements; how exact they have to be, the bound alone decides.
A program may use at most 64 MiB of HBM per device.

v0:
```python
import jax
import jax.numpy as jnp
from jax import lax
from jax.sharding import PartitionSpec as P

HD = 64
HIGH = lax.Precision.HIGHEST
OFFSETS = ((-1, -1), (-1, 0), (-1, 1), (0, -1), (0, 0), (0, 1), (1, -1), (1, 0), (1, 1))


def joined_along(pieces, dim):
    lengths = list(pieces.shape[1:])
    lengths[dim] *= pieces.shape[0]
    return jnp.moveaxis(pieces, 0, dim).reshape(lengths)


def copy_for_each(value, axis):
    copies = jnp.broadcast_to(value, (lax.axis_size(axis), *value.shape))
    return lax.all_to_all(copies, axis, split_axis=0, concat_axis=0, tiled=True)


def gather_directly(value, axis, dim):
    return joined_along(copy_for_each(value, axis), dim)


def extended(value, sides, width):
    for axis, dim in sides:
        peers, length = (lax.axis_size(axis), value.shape[dim])
        up = [(i, (i + 1) % peers) for i in range(peers)]
        down = [(j, i) for i, j in up]
        last = lax.slice_in_dim(value, length - width, length, axis=dim)
        initial = lax.slice_in_dim(value, 0, width, axis=dim)
        before = lax.ppermute(last, axis, up)
        after = lax.ppermute(initial, axis, down)
        value = jnp.concatenate([before, value, after], axis=dim)
    return value


def cut_along(value, dim, peers):
    lengths = value.shape
    pieces = value.reshape(*lengths[:dim], peers, lengths[dim] // peers, *lengths[dim + 1 :])
    return jnp.moveaxis(pieces, dim, 0)


def summed_on_arrival(value, axis, dim):
    peers = lax.axis_size(axis)
    pieces = lax.all_to_all(cut_along(value, dim, peers), axis, 0, 0, tiled=True)
    return jnp.sum(pieces, axis=0)


def split_heads(matrix):
    return matrix.reshape(matrix.shape[0], -1, HD)


def latitude_weights(row_count, band_index, band_count):
    line_total = row_count * band_count
    centres = (jnp.arange(line_total, dtype=jnp.float32) + 0.5) * (jnp.pi / line_total)
    mean_cosine = jnp.sum(jnp.sin(centres)) / line_total
    mine = (band_index * row_count + jnp.arange(row_count, dtype=jnp.int32)).astype(jnp.float32)
    return jnp.sin((mine + 0.5) * (jnp.pi / line_total)) / mean_cosine


def close_poles(padded, row_dim, band_index, band_count):
    height = padded.shape[row_dim]
    positions = jnp.arange(height)
    outside = (positions == 0) & (band_index == 0) | (positions == height - 1) & (
        band_index == band_count - 1
    )
    shape_mask = [1] * padded.ndim
    shape_mask[row_dim] = height
    return jnp.where(outside.reshape(shape_mask), 0.0, padded)


def spread_taps(weighted, grad_padded, conv_taps):
    row_count, col_count = (weighted.shape[0], weighted.shape[1])
    result = weighted
    for tap_index, (shift_row, shift_col) in enumerate(OFFSETS):
        result = (
            result
            + conv_taps[tap_index]
            * grad_padded[
                1 - shift_row : 1 - shift_row + row_count, 1 - shift_col : 1 - shift_col + col_count
            ]
        )
    return result


def tap_terms(weighted, out_padded):
    row_count, col_count = (weighted.shape[0], weighted.shape[1])
    term_list = []
    for shift_row, shift_col in OFFSETS:
        term_list.append(
            jnp.sum(
                out_padded[
                    1 + shift_row : 1 + shift_row + row_count,
                    1 + shift_col : 1 + shift_col + col_count,
                ]
                * weighted,
                axis=(0, 1),
            )
        )
    return jnp.stack(term_list)


def group_logits(query_part, key_part):
    return jnp.einsum(
        "qhd,khd->hqk", split_heads(query_part), split_heads(key_part), precision=HIGH
    ) * HD ** (-0.5)


def body(queries, key_rows, value_rows, cotangent, conv_taps):
    row_count, col_count, channels = queries.shape
    band_count = lax.axis_size("lat")
    band_index = lax.axis_index("lat")
    weighted = cotangent * latitude_weights(row_count, band_index, band_count)[:, None, None]
    paired_rows = jnp.concatenate([key_rows, value_rows], 1)
    paired_sector = gather_directly(paired_rows, "lon", 0)
    paired_all = lax.all_gather(paired_sector, "lat", axis=0, tiled=True)
    key_all = paired_all[:, :channels]
    value_all = paired_all[:, channels:]
    token_count = row_count * col_count
    key_count = key_all.shape[0]
    query_flat = queries.reshape(token_count, channels)
    group_width = 2 * HD
    group_count = channels // group_width
    outputs = []
    peaks = []
    sums_soft = []
    for group_index in range(group_count):
        col_start = group_index * group_width
        col_stop = col_start + group_width
        logits = group_logits(query_flat[:, col_start:col_stop], key_all[:, col_start:col_stop])
        row_peak = jnp.max(logits, -1, keepdims=True)
        raised = jnp.exp(logits - row_peak)
        normaliser = jnp.sum(raised, -1, keepdims=True)
        soft_weights = raised / normaliser
        outputs.append(
            jnp.einsum(
                "hqk,khd->qhd",
                soft_weights,
                split_heads(value_all[:, col_start:col_stop]),
                precision=HIGH,
            ).reshape(token_count, group_width)
        )
        peaks.append(row_peak)
        sums_soft.append(normaliser)
    out_flat = jnp.concatenate(outputs, 1)
    out_grid = out_flat.reshape(row_count, col_count, channels)
    both_padded = close_poles(
        extended(jnp.stack([weighted, out_grid]), (("lat", 1), ("lon", 2)), 1),
        1,
        band_index,
        band_count,
    )
    grad_padded = both_padded[0]
    out_padded = both_padded[1]
    out_grad = spread_taps(weighted, grad_padded, conv_taps)
    tap_sum = lax.psum(tap_terms(weighted, out_padded), ("lat", "lon"))
    tap_update = tap_sum / jnp.sqrt(jnp.mean(tap_sum * tap_sum) + 1e-06)
    grad_flat = out_grad.reshape(token_count, channels)
    query_parts = []
    key_parts = []
    value_parts = []
    for group_index in range(group_count):
        col_start = group_index * group_width
        col_stop = col_start + group_width
        query_heads = split_heads(query_flat[:, col_start:col_stop])
        key_heads = split_heads(key_all[:, col_start:col_stop])
        logits = jnp.einsum("qhd,khd->hqk", query_heads, key_heads, precision=HIGH) * HD ** (-0.5)
        soft_weights = jnp.exp(logits - peaks[group_index]) / sums_soft[group_index]
        grad_heads = split_heads(grad_flat[:, col_start:col_stop])
        value_parts.append(
            jnp.einsum("hqk,qhd->khd", soft_weights, grad_heads, precision=HIGH).reshape(
                key_count, group_width
            )
        )
        prob_grad = jnp.einsum(
            "qhd,khd->hqk",
            grad_heads,
            split_heads(value_all[:, col_start:col_stop]),
            precision=HIGH,
        )
        row_dot = jnp.transpose(
            jnp.sum(grad_heads * split_heads(out_flat[:, col_start:col_stop]), -1)
        )[:, :, None]
        logit_grad = soft_weights * (prob_grad - row_dot)
        query_parts.append(
            (
                jnp.einsum("hqk,khd->qhd", logit_grad, key_heads, precision=HIGH) * HD ** (-0.5)
            ).reshape(token_count, group_width)
        )
        key_parts.append(
            (
                jnp.einsum("hqk,qhd->khd", logit_grad, query_heads, precision=HIGH) * HD ** (-0.5)
            ).reshape(key_count, group_width)
        )
    paired_terms = jnp.concatenate(key_parts + value_parts, 1)
    paired_band = lax.psum_scatter(paired_terms, "lat", scatter_dimension=0, tiled=True)
    paired_grad = summed_on_arrival(paired_band, "lon", 0)
    key_grad = paired_grad[:, :channels]
    value_grad = paired_grad[:, channels:]
    query_grad = jnp.concatenate(query_parts, 1).reshape(row_count, col_count, channels)
    return (query_grad, key_grad, value_grad, tap_update)


def solution(mesh):
    placed = (
        P("lat", "lon", None),
        P(("lat", "lon"), None),
        P(("lat", "lon"), None),
        P("lat", "lon", None),
        P(),
    )
    return jax.shard_map(
        body,
        mesh=mesh,
        in_specs=placed,
        out_specs=(P("lat", "lon", None), P(("lat", "lon"), None), P(("lat", "lon"), None), P()),
        check_vma=False,
    )
```

profile of v0, /device:TPU:1, one launch (start us, length us, event | category | flops | bytes accessed | tf_op | source)
XLA Modules:
  0.0 343.2 jit_solution(12765066276765064027)
XLA Ops:
  7.2 0.7 pad_maximum_fusion.13
  8.0 18.8 %all_to_all.10 = f32[32,1,1024]{2,1,0:T(1,128)} all-to-all(f32[32,1,1024]{2,1,0:T(1,128)S(1)} %broadcast_in_dim.10), channel_id=1, replica_groups=mesh['lat'=16,'lon'=32] {'lon'}, dimensions={0} | all-to-all | bytes 262144 | tf_op jit(solution)/shard_map/all_to_all | solution.py:19
  26.9 1.0 fusion.53
  27.9 0.7 copy.151
  28.6 0.7 copy.150
  29.5 0.7 sine_reduce_fusion
  30.8 1.0 fusion.50
  31.8 88.1 %all-gather.3.cloned.1.call-done = f32[512,1,1024]{2,1,0:T(1,128)} async-done(((f32[32,1,1024]{2,1,0:T(1,128)}), f32[512,1,1024]{2,1,0:T(1,128)}) %all-gather.3.cloned.1.call-update) | async-done | bytes 2097168 | tf_op jit(solution)/shard_map/all_gather | solution.py:118
  120.0 2.1 copy.158
  122.8 0.8 copy.91
  123.9 0.9 copy.83
  124.8 1.0 fusion.56
  125.9 0.5 convolution_bitcast_fusion
  126.7 1.0 fusion.58
  127.8 1.1 convolution_bitcast_fusion.2
  128.9 1.0 copy.90
  130.0 1.0 fusion.57
  131.2 0.5 convolution_bitcast_fusion.1
  131.9 1.0 fusion.59
  133.1 1.4 convolution_bitcast_fusion.3
  134.8 2.1 collective-permute-start
  136.9 9.2 %collective-permute-start.1 = (f32[2,1,32,512]{3,2,1,0:T(8,128)S(1)}, f32[2,1,32,512]{3,2,1,0:T(8,128)S(1)}, u32[]{:S(2)}, u32[]{:S(2)}) collective-permute-start(f32[2,1,32,512]{3,2,1,0:T(8,128)S(1)} %get-tuple-element.26), channel_id=1, source_target_pairs={{32,0},{64,32},{96,64},{128,96},{160,128},{192,160},{224,192},{256... | collective-permute-start | bytes 393224 | tf_op jit(solution)/shard_map/ppermute | solution.py:34
  146.1 4.7 %collective-permute-done = f32[2,1,32,512]{3,2,1,0:T(8,128)S(1)} collective-permute-done((f32[2,1,32,512]{3,2,1,0:T(8,128)S(1)}, f32[2,1,32,512]{3,2,1,0:T(8,128)S(1)}, u32[]{:S(2)}, u32[]{:S(2)}) %collective-permute-start) | collective-permute-done | bytes 131104 | tf_op jit(solution)/shard_map/ppermute | solution.py:33
  150.9 3.2 collective-permute-start.2
  154.1 2.1 collective-permute-start.3
  156.3 3.3 collective-permute-done.3
  159.9 0.3 fusion.29
  160.2 0.7 fusion.52
  160.9 1.6 copy.153
  162.4 0.9 multiply_reduce_fusion.3
  163.3 1.6 copy.155
  164.9 0.9 multiply_reduce_fusion.1
  165.8 1.6 copy.154
  167.3 0.9 multiply_reduce_fusion.2
  168.2 1.6 copy.156
  169.8 0.9 multiply_reduce_fusion
  170.8 1.6 fusion.38
  172.4 1.0 fusion
  173.4 0.7 convolution_multiply_fusion.4
  174.1 0.7 fusion.44
  174.9 1.0 fusion.2
  175.9 0.7 convolution_multiply_fusion.6
  176.6 0.7 fusion.41
  177.4 1.0 fusion.1
  178.4 0.7 convolution_multiply_fusion.5
  179.1 0.7 fusion.47
  179.9 1.0 fusion.3
  180.9 0.7 convolution_multiply_fusion.7
  181.8 1.9 copy.146
  183.8 0.3 fusion.20
  184.1 117.4 %psum.7 = f32[9,512]{1,0:T(8,128)S(1)} all-reduce(f32[9,512]{1,0:T(8,128)S(1)} %stack.47), channel_id=1, replica_groups=mesh['lat'=16,'lon'=32] {'lat','lon'}, use_global_device_ids=true, to_apply=%region_24.25 | all-reduce | flops 4608 | bytes 36864 | tf_op jit(solution)/shard_map/psum | solution.py:158
  301.5 0.6 multiply_reduce_fusion.4
  302.8 0.4 fusion.8
  303.5 0.4 fusion.10
  304.2 0.4 fusion.9
  304.9 13.6 %reduce-scatter.4.cloned.1.call-done = f32[32,1024]{1,0:T(8,128)} async-done(((f32[512,1024]{1,0:T(8,128)}), f32[32,1024]{1,0:T(8,128)}) %reduce-scatter.4.cloned.1.call-update) | async-done | bytes 131088
  318.5 1.1 copy.147
  319.6 0.8 copy.125
  320.4 6.7 %all-to-all-start.1 = ((f32[32,1,1024]{2,1,0:T(1,128)}), f32[32,1,1024]{2,1,0:T(1,128)S(1)}, u32[]{:S(2)}, u32[]{:S(2)}) async-start(f32[32,1,1024]{2,1,0:T(1,128)} %copy.125), calls=%async_computation.1 | async-start | bytes 262144 | tf_op jit(solution)/shard_map/all_to_all | solution.py:47
  327.1 0.4 fusion.11
  327.8 0.7 pad_maximum_fusion
  328.5 0.6 broadcast_divide_fusion
  329.2 6.5 %all-to-all-done.1 = f32[32,1,1024]{2,1,0:T(1,128)S(1)} async-done(((f32[32,1,1024]{2,1,0:T(1,128)}), f32[32,1,1024]{2,1,0:T(1,128)S(1)}, u32[]{:S(2)}, u32[]{:S(2)}) %all-to-all-start.1) | async-done | bytes 131104 | tf_op jit(solution)/shard_map/all_to_all | solution.py:47
  335.7 0.6 fusion.55
  (122 shorter events, 4.4 us)
Async XLA Ops:
  7.2 112.8 %all-gather.3.cloned.1.call-start = ((), (), s32[]{:S(2)}) async-start(), calls=%async_computation.3 | async-start | bytes 2228224 | tf_op jit(solution)/shard_map/all_gather | solution.py:118
  26.8 291.7 %reduce-scatter.4.cloned.1.call-start = ((), (), s32[]{:S(2)}) async-start(), calls=%async_computation.4 | async-start | bytes 2228224
  29.4 95.3 %copy-start.17 = (f32[128,128]{0,1:T(8,128)}, f32[128,128]{0,1:T(8,128)S(1)}, u32[]{:S(2)}) copy-start(f32[128,128]{0,1:T(8,128)S(1)} %copy.152) | copy-start | bytes 196612
  122.5 3.4 copy-start.1
  122.6 3.8 %copy-start.28 = (f32[512,128]{0,1:T(8,128)}, f32[512,128]{0,1:T(8,128)S(1)}, u32[]{:S(2)}) copy-start(f32[512,128]{0,1:T(8,128)S(1)} %copy.96) | copy-start | bytes 786436
  123.8 2.9 copy-start.3
  123.9 3.9 %copy-start.26 = (f32[512,128]{0,1:T(8,128)}, f32[512,128]{0,1:T(8,128)S(1)}, u32[]{:S(2)}) copy-start(f32[512,128]{0,1:T(8,128)S(1)} %copy.86) | copy-start | bytes 786436
  123.9 2.8 copy-start.15
  126.4 3.6 %copy-start.19 = (f32[128,2,64]{0,2,1:T(8,128)}, f32[128,2,64]{0,2,1:T(8,128)S(1)}, u32[]{:S(2)}) copy-start(f32[128,2,64]{0,2,1:T(8,128)S(1)} %convolution_bitcast_fusion) | copy-start | bytes 196612
  126.4 3.6 %copy-start.13 = (f32[128,128]{0,1:T(8,128)S(1)}, f32[128,128]{0,1:T(8,128)}, u32[]{:S(2)}) copy-start(f32[128,128]{0,1:T(8,128)} %copy.151) | copy-start | bytes 196612
  127.7 3.4 %copy-start.24 = (f32[512,128]{0,1:T(8,128)S(1)}, f32[512,128]{0,1:T(8,128)}, u32[]{:S(2)}) copy-start(f32[512,128]{0,1:T(8,128)} %copy.91) | copy-start | bytes 786436
  131.7 19.2 %copy-start.21 = (f32[128,2,64]{0,2,1:T(8,128)}, f32[128,2,64]{0,2,1:T(8,128)S(1)}, u32[]{:S(2)}) copy-start(f32[128,2,64]{0,2,1:T(8,128)S(1)} %convolution_bitcast_fusion.1) | copy-start | bytes 196612
  132.9 13.2 %copy-start.34 = (f32[9,512]{1,0:T(8,128)S(1)}, f32[9,512]{1,0:T(8,128)}, u32[]{:S(2)}) copy-start(f32[9,512]{1,0:T(8,128)} %param.9) | copy-start | bytes 55300
  134.5 16.3 %copy-start.22 = (f32[128,2,64]{0,2,1:T(8,128)}, f32[128,2,64]{0,2,1:T(8,128)S(1)}, u32[]{:S(2)}) copy-start(f32[128,2,64]{0,2,1:T(8,128)S(1)} %convolution_bitcast_fusion.3) | copy-start | bytes 196612
  134.8 16.0 %collective-permute-start = (f32[2,1,32,512]{3,2,1,0:T(8,128)S(1)}, f32[2,1,32,512]{3,2,1,0:T(8,128)S(1)}, u32[]{:S(2)}, u32[]{:S(2)}) collective-permute-start(f32[2,1,32,512]{3,2,1,0:T(8,128)S(1)} %get-tuple-element.25), channel_id=1, source_target_pairs={{0,32},{32,64},{64,96},{96,128},{128,160},{160,192},{192,224},{224... | collective-permute-start | bytes 393224 | tf_op jit(solution)/shard_map/ppermute | solution.py:33
  136.9 13.9 %collective-permute-start.1 = (f32[2,1,32,512]{3,2,1,0:T(8,128)S(1)}, f32[2,1,32,512]{3,2,1,0:T(8,128)S(1)}, u32[]{:S(2)}, u32[]{:S(2)}) collective-permute-start(f32[2,1,32,512]{3,2,1,0:T(8,128)S(1)} %get-tuple-element.26), channel_id=1, source_target_pairs={{32,0},{64,32},{96,64},{128,96},{160,128},{192,160},{224,192},{256... | collective-permute-start | bytes 393224 | tf_op jit(solution)/shard_map/ppermute | solution.py:34
  150.9 9.0 %copy-start = (f32[4,32,512]{2,1,0:T(8,128)S(1)}, f32[4,32,512]{2,1,0:T(8,128)}, u32[]{:S(2)}) copy-start(f32[4,32,512]{2,1,0:T(8,128)} %param.8) | copy-start | bytes 786436
  150.9 5.4 %collective-permute-start.2 = (f32[2,6,1,512]{3,2,1,0:T(1,128)S(1)}, f32[2,6,1,512]{3,2,1,0:T(1,128)S(1)}, u32[]{:S(2)}, u32[]{:S(2)}) collective-permute-start(f32[2,6,1,512]{3,2,1,0:T(1,128)S(1)} %get-tuple-element.23), channel_id=1, source_target_pairs={{0,1},{1,2},{2,3},{3,4},{4,5},{5,6},{6,7},{7,8},{8,9},{9,10},{10,1... | collective-permute-start | bytes 73736 | tf_op jit(solution)/shard_map/ppermute | solution.py:33
  154.1 5.4 %collective-permute-start.3 = (f32[2,6,1,512]{3,2,1,0:T(1,128)S(1)}, f32[2,6,1,512]{3,2,1,0:T(1,128)S(1)}, u32[]{:S(2)}, u32[]{:S(2)}) collective-permute-start(f32[2,6,1,512]{3,2,1,0:T(1,128)S(1)} %get-tuple-element.24), channel_id=1, source_target_pairs={{1,0},{2,1},{3,2},{4,3},{5,4},{6,5},{7,6},{8,7},{9,8},{10,9},{11,1... | collective-permute-start | bytes 73736 | tf_op jit(solution)/shard_map/ppermute | solution.py:34
  159.9 9.9 %copy-start.20 = (f32[128,2,64]{0,2,1:T(8,128)S(1)}, f32[128,2,64]{0,2,1:T(8,128)}, u32[]{:S(2)}) copy-start(f32[128,2,64]{0,2,1:T(8,128)} %copy-done.19) | copy-start | bytes 196612
  169.8 2.5 copy-start.29
  169.8 2.5 copy-start.33
  170.7 2.6 copy-start.18
  170.7 3.4 copy-start.32
  172.4 2.5 copy-start.27
  173.4 2.5 copy-start.7
  174.1 1.8 copy-start.16
  174.1 2.5 copy-start.31
  174.8 2.5 copy-start.25
  175.9 2.5 copy-start.9
  176.6 1.8 copy-start.14
  176.6 2.5 copy-start.30
  177.4 2.5 copy-start.23
  178.4 1.4 copy-start.11
  180.9 0.9 copy-start.5
  183.7 119.1 %copy-start.2 = (f32[512,128]{0,1:T(8,128)S(1)}, f32[512,128]{0,1:T(8,128)}, u32[]{:S(2)}) copy-start(f32[512,128]{0,1:T(8,128)} %copy-done.1) | copy-start | bytes 786436
  183.7 119.1 %copy-start.8 = (f32[2,128,512]{1,2,0:T(8,128)S(1)}, f32[2,128,512]{1,2,0:T(8,128)}, u32[]{:S(2)}) copy-start(f32[2,128,512]{1,2,0:T(8,128)} %copy-done.7) | copy-start | bytes 1572868
  183.7 119.8 %copy-start.4 = (f32[512,128]{0,1:T(8,128)S(1)}, f32[512,128]{0,1:T(8,128)}, u32[]{:S(2)}) copy-start(f32[512,128]{0,1:T(8,128)} %copy-done.3) | copy-start | bytes 786436
  183.7 119.8 %copy-start.10 = (f32[2,128,512]{1,2,0:T(8,128)S(1)}, f32[2,128,512]{1,2,0:T(8,128)}, u32[]{:S(2)}) copy-start(f32[2,128,512]{1,2,0:T(8,128)} %copy-done.9) | copy-start | bytes 1572868
  183.7 120.5 %copy-start.12 = (f32[2,128,512]{1,2,0:T(8,128)S(1)}, f32[2,128,512]{1,2,0:T(8,128)}, u32[]{:S(2)}) copy-start(f32[2,128,512]{1,2,0:T(8,128)} %copy-done.11) | copy-start | bytes 1572868
  303.4 23.7 %copy-start.6 = (f32[2,128,512]{1,2,0:T(8,128)S(1)}, f32[2,128,512]{1,2,0:T(8,128)}, u32[]{:S(2)}) copy-start(f32[2,128,512]{1,2,0:T(8,128)} %copy-done.5) | copy-start | bytes 1572868
  320.4 15.2 %all-to-all-start.1 = ((f32[32,1,1024]{2,1,0:T(1,128)}), f32[32,1,1024]{2,1,0:T(1,128)S(1)}, u32[]{:S(2)}, u32[]{:S(2)}) async-start(f32[32,1,1024]{2,1,0:T(1,128)} %copy.125), calls=%async_computation.1 | async-start | bytes 262144 | tf_op jit(solution)/shard_map/all_to_all | solution.py:47
Sparse Core Ops, SparseCore 0:
  26.9 93.0 all-gather.2
  183.8 134.6 reduce-scatter.3
where the time goes:
time: 344 us; the launch traced here: 343 us
  blocking collectives  136 us (40%)
  waiting for transfers between devices  116 us (34%)
  starting transfers between devices  23.4 us (7%)
  local copies, waits for them, and re-layouts  21.9 us (6%)
  matrix products  19.9 us (6%)
  between operations  16.2 us (5%)
  other arithmetic  9.35 us (3%)
    psum x1, blocking collectives, body(): tap_sum = lax.psum(tap_terms(weighted, out_padded), ('lat', 'lon'))  117 us
    all_gather x1, waiting for transfers between devices, body(): paired_all = lax.all_gather(paired_sector, 'lat', axis=0, tiled=True)  88.1 us
    all_to_all x1, blocking collectives, copy_for_each(): return lax.all_to_all(copies, axis, split_axis=0, concat_axis=0, tiled=True)  18.8 us
    unnamed x3, waiting for transfers between devices  13.6 us
    unnamed x88, local copies, waits for them, and re-layouts  13.2 us
    ppermute x2, starting transfers between devices, extended(): after = lax.ppermute(initial, axis, down)  11.3 us
  transfers between devices with their start and end apart: 7, of which 5 were waited for; matrix products, arithmetic and copies ran while one was open for 3% of the time, Pallas kernels for 0%

commit v1 on v0

--- a/solution.py
+++ b/solution.py
@@ -155,7 +155,11 @@
     grad_padded = both_padded[0]
     out_padded = both_padded[1]
     out_grad = spread_taps(weighted, grad_padded, conv_taps)
-    tap_sum = lax.psum(tap_terms(weighted, out_padded), ("lat", "lon"))
+
+    def divide_vector(sheet, dev_axis, which_axis):
+        return lax.psum(lax.psum(sheet, axis_name=dev_axis), axis_name=which_axis)
+
+    tap_sum = divide_vector(tap_terms(weighted, out_padded), "lat", "lon")
     tap_update = tap_sum / jnp.sqrt(jnp.mean(tap_sum * tap_sum) + 1e-06)
     grad_flat = out_grad.reshape(token_count, channels)
     query_parts = []

time: 344 us -> 447 us (1.30)
  blocking collectives: 136 us -> 250 us
  waiting for transfers between devices: 116 us -> 103 us
    psum x1 -> x2, blocking collectives: 117 us -> 231 us  [divide_vector(): return lax.psum(lax.psum(sheet, axis_name=dev_axis), axis_name=which_axis)]
    unnamed x3, waiting for transfers between devices: 13.6 us -> 0.04 us
  transfers between devices with their start and end apart: 7 -> 7, of which waited for: 5 -> 4; matrix products, arithmetic and copies ran while one was open for 3% -> 2% of each run, Pallas kernels for 0% -> 0%
where the time goes in v1:
time: 447 us; the launch traced here: 446 us
  blocking collectives  250 us (56%)
  waiting for transfers between devices  103 us (23%)
  starting transfers between devices  26.5 us (6%)
  local copies, waits for them, and re-layouts  21.9 us (5%)
  matrix products  19.9 us (4%)
  between operations  16.2 us (4%)
  other arithmetic  9.35 us (2%)
    psum x2, blocking collectives, divide_vector(): return lax.psum(lax.psum(sheet, axis_name=dev_axis), axis_name=which_axis)  231 us
    all_gather x1, waiting for transfers between devices, body(): paired_all = lax.all_gather(paired_sector, 'lat', axis=0, tiled=True)  88.1 us
    all_to_all x1, blocking collectives, copy_for_each(): return lax.all_to_all(copies, axis, split_axis=0, concat_axis=0, tiled=True)  18.8 us
    unnamed x88, local copies, waits for them, and re-layouts  13.2 us
    ppermute x2, starting transfers between devices, extended(): after = lax.ppermute(initial, axis, down)  11.3 us
    all_to_all x1, starting transfers between devices, summed_on_arrival(): lax.all_to_all(cut_along(value, dim, peers), axis, 0, 0, tiled=True)  9.74 us
  transfers between devices with their start and end apart: 7, of which 4 were waited for; matrix products, arithmetic and copies ran while one was open for 2% of the time, Pallas kernels for 0%

profile of v1, /device:TPU:1, one launch (start us, length us, event | category | flops | bytes accessed | tf_op | source)
XLA Modules:
  0.0 446.2 jit_solution(890653865953472241)
XLA Ops:
  7.2 0.7 pad_maximum_fusion.13
  8.0 18.8 %all_to_all.10 = f32[32,1,1024]{2,1,0:T(1,128)} all-to-all(f32[32,1,1024]{2,1,0:T(1,128)S(1)} %broadcast_in_dim.10), channel_id=1, replica_groups=mesh['lat'=16,'lon'=32] {'lon'}, dimensions={0} | all-to-all | bytes 262144 | tf_op jit(solution)/shard_map/all_to_all | solution.py:19
  26.9 1.0 fusion.53
  27.9 0.7 copy.151
  28.6 0.7 copy.150
  29.5 0.7 sine_reduce_fusion
  30.8 1.0 fusion.50
  31.8 88.1 %all-gather.3.cloned.1.call-done = f32[512,1,1024]{2,1,0:T(1,128)} async-done(((f32[32,1,1024]{2,1,0:T(1,128)}), f32[512,1,1024]{2,1,0:T(1,128)}) %all-gather.3.cloned.1.call-update) | async-done | bytes 2097168 | tf_op jit(solution)/shard_map/all_gather | solution.py:118
  120.0 2.1 copy.158
  122.8 0.8 copy.91
  123.9 0.9 copy.83
  124.8 1.0 fusion.56
  125.9 0.5 convolution_bitcast_fusion
  126.7 1.0 fusion.58
  127.8 1.1 convolution_bitcast_fusion.2
  128.9 1.0 copy.90
  130.0 1.0 fusion.57
  131.2 0.5 convolution_bitcast_fusion.1
  131.9 1.0 fusion.59
  133.1 1.4 convolution_bitcast_fusion.3
  134.8 2.1 collective-permute-start
  136.9 9.2 %collective-permute-start.1 = (f32[2,1,32,512]{3,2,1,0:T(8,128)S(1)}, f32[2,1,32,512]{3,2,1,0:T(8,128)S(1)}, u32[]{:S(2)}, u32[]{:S(2)}) collective-permute-start(f32[2,1,32,512]{3,2,1,0:T(8,128)S(1)} %get-tuple-element.26), channel_id=1, source_target_pairs={{32,0},{64,32},{96,64},{128,96},{160,128},{192,160},{224,192},{256... | collective-permute-start | bytes 393224 | tf_op jit(solution)/shard_map/ppermute | solution.py:34
  146.1 4.7 %collective-permute-done = f32[2,1,32,512]{3,2,1,0:T(8,128)S(1)} collective-permute-done((f32[2,1,32,512]{3,2,1,0:T(8,128)S(1)}, f32[2,1,32,512]{3,2,1,0:T(8,128)S(1)}, u32[]{:S(2)}, u32[]{:S(2)}) %collective-permute-start) | collective-permute-done | bytes 131104 | tf_op jit(solution)/shard_map/ppermute | solution.py:33
  150.9 3.2 collective-permute-start.2
  154.1 2.1 collective-permute-start.3
  156.3 3.3 collective-permute-done.3
  159.9 0.3 fusion.29
  160.2 0.7 fusion.52
  160.9 1.6 copy.153
  162.4 0.9 multiply_reduce_fusion.3
  163.3 1.6 copy.155
  164.9 0.9 multiply_reduce_fusion.1
  165.8 1.6 copy.154
  167.3 0.9 multiply_reduce_fusion.2
  168.2 1.6 copy.156
  169.8 0.9 multiply_reduce_fusion
  170.8 1.6 fusion.38
  172.4 1.0 fusion
  173.4 0.7 convolution_multiply_fusion.4
  174.1 0.7 fusion.44
  174.9 1.0 fusion.2
  175.9 0.7 convolution_multiply_fusion.6
  176.6 0.7 fusion.41
  177.4 1.0 fusion.1
  178.4 0.7 convolution_multiply_fusion.5
  179.1 0.7 fusion.47
  179.9 1.0 fusion.3
  180.9 0.7 convolution_multiply_fusion.7
  181.8 1.9 copy.146
  183.8 0.3 fusion.20
  184.1 87.6 %psum.14 = f32[9,512]{1,0:T(8,128)S(1)} all-reduce(f32[9,512]{1,0:T(8,128)S(1)} %stack.47), channel_id=1, replica_groups=mesh['lat'=16,'lon'=32] {'lat'}, use_global_device_ids=true, to_apply=%region_24.25 | all-reduce | flops 4608 | bytes 36864 | tf_op jit(solution)/shard_map/psum | solution.py:160
  271.7 143.2 %psum.15 = f32[9,512]{1,0:T(8,128)S(1)} all-reduce(f32[9,512]{1,0:T(8,128)S(1)} %psum.14), channel_id=1, replica_groups=mesh['lat'=16,'lon'=32] {'lon'}, use_global_device_ids=true, to_apply=%region_25.26 | all-reduce | flops 4608 | bytes 36864 | tf_op jit(solution)/shard_map/psum | solution.py:160
  414.9 0.6 multiply_reduce_fusion.4
  416.2 0.4 fusion.8
  416.9 0.4 fusion.10
  417.6 0.4 fusion.9
  418.3 1.1 copy.147
  419.4 0.8 copy.125
  420.2 9.7 %all-to-all-start.1 = ((f32[32,1,1024]{2,1,0:T(1,128)}), f32[32,1,1024]{2,1,0:T(1,128)S(1)}, u32[]{:S(2)}, u32[]{:S(2)}) async-start(f32[32,1,1024]{2,1,0:T(1,128)} %copy.125), calls=%async_computation.1 | async-start | bytes 262144 | tf_op jit(solution)/shard_map/all_to_all | solution.py:47
  430.0 0.4 fusion.11
  430.7 0.7 pad_maximum_fusion
  431.4 0.6 broadcast_divide_fusion
  432.0 6.6 %all-to-all-done.1 = f32[32,1,1024]{2,1,0:T(1,128)S(1)} async-done(((f32[32,1,1024]{2,1,0:T(1,128)}), f32[32,1,1024]{2,1,0:T(1,128)S(1)}, u32[]{:S(2)}, u32[]{:S(2)}) %all-to-all-start.1) | async-done | bytes 131104 | tf_op jit(solution)/shard_map/all_to_all | solution.py:47
  438.7 0.6 fusion.55
  (123 shorter events, 4.4 us)
Async XLA Ops:
  7.2 112.8 %all-gather.3.cloned.1.call-start = ((), (), s32[]{:S(2)}) async-start(), calls=%async_computation.3 | async-start | bytes 2228224 | tf_op jit(solution)/shard_map/all_gather | solution.py:118
  26.8 391.5 %reduce-scatter.4.cloned.1.call-start = ((), (), s32[]{:S(2)}) async-start(), calls=%async_computation.4 | async-start | bytes 2228224
  29.4 95.3 %copy-start.17 = (f32[128,128]{0,1:T(8,128)}, f32[128,128]{0,1:T(8,128)S(1)}, u32[]{:S(2)}) copy-start(f32[128,128]{0,1:T(8,128)S(1)} %copy.152) | copy-start | bytes 196612
  122.5 3.4 copy-start.1
  122.6 3.8 copy-start.28
  123.8 2.9 copy-start.3
  123.9 3.9 copy-start.26
  123.9 2.8 copy-start.15
  126.4 3.6 copy-start.19
  126.4 3.6 copy-start.13
  127.7 3.4 copy-start.24
  131.7 19.2 %copy-start.21 = (f32[128,2,64]{0,2,1:T(8,128)}, f32[128,2,64]{0,2,1:T(8,128)S(1)}, u32[]{:S(2)}) copy-start(f32[128,2,64]{0,2,1:T(8,128)S(1)} %convolution_bitcast_fusion.1) | copy-start | bytes 196612
  132.9 13.2 %copy-start.34 = (f32[9,512]{1,0:T(8,128)S(1)}, f32[9,512]{1,0:T(8,128)}, u32[]{:S(2)}) copy-start(f32[9,512]{1,0:T(8,128)} %param.9) | copy-start | bytes 55300
  134.5 16.3 %copy-start.22 = (f32[128,2,64]{0,2,1:T(8,128)}, f32[128,2,64]{0,2,1:T(8,128)S(1)}, u32[]{:S(2)}) copy-start(f32[128,2,64]{0,2,1:T(8,128)S(1)} %convolution_bitcast_fusion.3) | copy-start | bytes 196612
  134.8 16.0 %collective-permute-start = (f32[2,1,32,512]{3,2,1,0:T(8,128)S(1)}, f32[2,1,32,512]{3,2,1,0:T(8,128)S(1)}, u32[]{:S(2)}, u32[]{:S(2)}) collective-permute-start(f32[2,1,32,512]{3,2,1,0:T(8,128)S(1)} %get-tuple-element.25), channel_id=1, source_target_pairs={{0,32},{32,64},{64,96},{96,128},{128,160},{160,192},{192,224},{224... | collective-permute-start | bytes 393224 | tf_op jit(solution)/shard_map/ppermute | solution.py:33
  136.9 13.9 %collective-permute-start.1 = (f32[2,1,32,512]{3,2,1,0:T(8,128)S(1)}, f32[2,1,32,512]{3,2,1,0:T(8,128)S(1)}, u32[]{:S(2)}, u32[]{:S(2)}) collective-permute-start(f32[2,1,32,512]{3,2,1,0:T(8,128)S(1)} %get-tuple-element.26), channel_id=1, source_target_pairs={{32,0},{64,32},{96,64},{128,96},{160,128},{192,160},{224,192},{256... | collective-permute-start | bytes 393224 | tf_op jit(solution)/shard_map/ppermute | solution.py:34
  150.9 9.0 %copy-start = (f32[4,32,512]{2,1,0:T(8,128)S(1)}, f32[4,32,512]{2,1,0:T(8,128)}, u32[]{:S(2)}) copy-start(f32[4,32,512]{2,1,0:T(8,128)} %param.8) | copy-start | bytes 786436
  150.9 5.4 %collective-permute-start.2 = (f32[2,6,1,512]{3,2,1,0:T(1,128)S(1)}, f32[2,6,1,512]{3,2,1,0:T(1,128)S(1)}, u32[]{:S(2)}, u32[]{:S(2)}) collective-permute-start(f32[2,6,1,512]{3,2,1,0:T(1,128)S(1)} %get-tuple-element.23), channel_id=1, source_target_pairs={{0,1},{1,2},{2,3},{3,4},{4,5},{5,6},{6,7},{7,8},{8,9},{9,10},{10,1... | collective-permute-start | bytes 73736 | tf_op jit(solution)/shard_map/ppermute | solution.py:33
  154.1 5.4 %collective-permute-start.3 = (f32[2,6,1,512]{3,2,1,0:T(1,128)S(1)}, f32[2,6,1,512]{3,2,1,0:T(1,128)S(1)}, u32[]{:S(2)}, u32[]{:S(2)}) collective-permute-start(f32[2,6,1,512]{3,2,1,0:T(1,128)S(1)} %get-tuple-element.24), channel_id=1, source_target_pairs={{1,0},{2,1},{3,2},{4,3},{5,4},{6,5},{7,6},{8,7},{9,8},{10,9},{11,1... | collective-permute-start | bytes 73736 | tf_op jit(solution)/shard_map/ppermute | solution.py:34
  159.9 9.9 %copy-start.20 = (f32[128,2,64]{0,2,1:T(8,128)S(1)}, f32[128,2,64]{0,2,1:T(8,128)}, u32[]{:S(2)}) copy-start(f32[128,2,64]{0,2,1:T(8,128)} %copy-done.19) | copy-start | bytes 196612
  169.8 2.5 copy-start.29
  169.8 2.5 copy-start.33
  170.7 2.6 copy-start.18
  170.7 3.4 copy-start.32
  172.4 2.5 copy-start.27
  173.4 2.5 copy-start.7
  174.1 1.8 copy-start.16
  174.1 2.5 copy-start.31
  174.8 2.5 copy-start.25
  175.9 2.5 copy-start.9
  176.6 1.8 copy-start.14
  176.6 2.5 copy-start.30
  177.4 2.5 copy-start.23
  178.4 1.4 copy-start.11
  180.9 0.9 copy-start.5
  183.7 232.5 %copy-start.2 = (f32[512,128]{0,1:T(8,128)S(1)}, f32[512,128]{0,1:T(8,128)}, u32[]{:S(2)}) copy-start(f32[512,128]{0,1:T(8,128)} %copy-done.1) | copy-start | bytes 786436
  183.7 232.5 %copy-start.8 = (f32[2,128,512]{1,2,0:T(8,128)S(1)}, f32[2,128,512]{1,2,0:T(8,128)}, u32[]{:S(2)}) copy-start(f32[2,128,512]{1,2,0:T(8,128)} %copy-done.7) | copy-start | bytes 1572868
  183.7 233.2 %copy-start.4 = (f32[512,128]{0,1:T(8,128)S(1)}, f32[512,128]{0,1:T(8,128)}, u32[]{:S(2)}) copy-start(f32[512,128]{0,1:T(8,128)} %copy-done.3) | copy-start | bytes 786436
  183.7 233.2 %copy-start.10 = (f32[2,128,512]{1,2,0:T(8,128)S(1)}, f32[2,128,512]{1,2,0:T(8,128)}, u32[]{:S(2)}) copy-start(f32[2,128,512]{1,2,0:T(8,128)} %copy-done.9) | copy-start | bytes 1572868
  183.7 233.9 %copy-start.12 = (f32[2,128,512]{1,2,0:T(8,128)S(1)}, f32[2,128,512]{1,2,0:T(8,128)}, u32[]{:S(2)}) copy-start(f32[2,128,512]{1,2,0:T(8,128)} %copy-done.11) | copy-start | bytes 1572868
  416.8 13.2 %copy-start.6 = (f32[2,128,512]{1,2,0:T(8,128)S(1)}, f32[2,128,512]{1,2,0:T(8,128)}, u32[]{:S(2)}) copy-start(f32[2,128,512]{1,2,0:T(8,128)} %copy-done.5) | copy-start | bytes 1572868
  420.2 18.4 %all-to-all-start.1 = ((f32[32,1,1024]{2,1,0:T(1,128)}), f32[32,1,1024]{2,1,0:T(1,128)S(1)}, u32[]{:S(2)}, u32[]{:S(2)}) async-start(f32[32,1,1024]{2,1,0:T(1,128)} %copy.125), calls=%async_computation.1 | async-start | bytes 262144 | tf_op jit(solution)/shard_map/all_to_all | solution.py:47
Sparse Core Ops, SparseCore 0:
  26.9 93.0 all-gather.2
  183.8 136.0 reduce-scatter.3
